TPU v7x, 32 devices: a whole 2x2x4 slice. The times are simulated.
32 devices in a mesh: seq: 8 (over z, x), exp: 4 (over y, core).
Axes of the slice: x: 2, y: 2, z: 4, core: 2. Of those that a mesh axis runs over, the one named last changes fastest.
Arguments:
- block_input: float32 [4096, 768], P(('seq', 'exp')), may hold values from -6 to 6
- seq_lengths: int32 [10], replicated, may hold values from 1 to 2048, 4096 in all
- expert_ids: int32 [4096, 1], P(('seq', 'exp')), may hold values from 0 to 3
- output_grad: float32 [4096, 768], P(('seq', 'exp')), may hold values from -6 to 6
- mixer_gain: float32 [768], replicated, may hold values from 0.5 to 1.5
- in_proj: float32 [768, 3072], replicated, may hold values from -0.21875 to 0.21875
- conv_weight: float32 [4, 1536], replicated, may hold values from -3 to 3
- conv_bias: float32 [1536], replicated, may hold values from -1.75 to 1.75
- state_proj: float32 [1536, 80], replicated, may hold values from -0.15625 to 0.15625
- step_proj: float32 [48, 1536], replicated, may hold values from -0.875 to 0.875
- step_bias: float32 [1536], replicated, may hold values from -7 to -2.5
- decay_log: float32 [1536, 16], replicated, may hold values from 0 to 2.77
- skip_gain: float32 [1536], replicated, may hold values from 0.5 to 1.5
- out_proj: float32 [1536, 768], replicated, may hold values from -0.3125 to 0.3125
- router_gain: float32 [768], replicated, may hold values from 0.5 to 1.5
- router: float32 [768, 4], replicated, may hold values from -0.15625 to 0.15625
- expert_up: float32 [4, 768, 3072], P('exp', None, 'seq'), may hold values from -0.21875 to 0.21875
- expert_down: float32 [4, 3072, 768], P('exp', 'seq'), may hold values from -0.875 to 0.875
Outputs:
- block_output: float32 [4096, 768], P(('seq', 'exp'))
- input_grad: float32 [4096, 768], P(('seq', 'exp'))
- grad_mixer_gain: float32 [768], replicated
- grad_in_proj: float32 [768, 3072], replicated
- grad_conv_weight: float32 [4, 1536], replicated
- grad_conv_bias: float32 [1536], replicated
- grad_state_proj: float32 [1536, 80], replicated
- grad_step_proj: float32 [48, 1536], replicated
- grad_step_bias: float32 [1536], replicated
- grad_decay_log: float32 [1536, 16], replicated
- grad_skip_gain: float32 [1536], replicated
- grad_out_proj: float32 [1536, 768], replicated
- grad_router_gain: float32 [768], replicated
- grad_router: float32 [768, 4], replicated
- grad_expert_up: float32 [4, 768, 3072], P('exp', None, 'seq')
- grad_expert_down: float32 [4, 3072, 768], P('exp', 'seq')
- expert_load: int32 [4], replicated
- dropped_load: int32 [4], replicated
All inputs are finite; a program needn't handle non-finite values.
Results may differ from a plain program's by a relative error of at most 0.0003.
Values sent between devices are 32-bit elements; how exact they have to be, the bound alone decides.
No kernel may reach another device: no remote copies, remote signals or barrier semaphores. Data moves between devices by JAX's collectives and lax.ppermute only.
A program may use at most 448 MiB of HBM per device.

v0:
```python
import jax
import jax.numpy as jnp
from jax import lax
from jax.sharding import PartitionSpec as P

precise = lax.Precision.HIGHEST
epsilon = 1e-05


def passed_along(block, axis, distance):
    devices = range(lax.axis_size(axis))
    route = [(i - distance, i) for i in devices if i - distance in devices]
    return lax.ppermute(block, axis, route)


def entering(value, axis, join, neutral, backward):
    count, mine = (lax.axis_size(axis), lax.axis_index(axis))
    pieces = jax.tree.map(lambda part: lax.all_gather(part, axis), value)
    if backward:
        pieces = jax.tree.map(lambda part: part[::-1], pieces)
        mine = count - 1 - mine
    so_far = jax.tree.map(
        lambda part, zero: jnp.full_like(part, 0) + jnp.asarray(zero, part.dtype), value, neutral
    )

    def lap(position, so_far):
        longer = join(so_far, jax.tree.map(lambda part: part[position], pieces))
        return jax.tree.map(lambda new, old: jnp.where(position < mine, new, old), longer, so_far)

    return lax.fori_loop(0, count - 1, lap, so_far)


def matmul_high(left, right):
    return jnp.dot(left, right, precision=precise, preferred_element_type=jnp.float32)


def rms_scale(values_in, gain):
    return (
        values_in
        * lax.rsqrt(jnp.mean(values_in * values_in, axis=1, keepdims=True) + epsilon)
        * gain
    )


def chain_states(earlier, later):
    return (later[0] * earlier[0], later[0] * earlier[1] + later[1])


def per_device(
    block_input,
    seq_lengths,
    expert_ids,
    output_grad,
    mixer_gain,
    in_proj,
    conv_weight,
    conv_bias,
    state_proj,
    step_proj,
    step_bias,
    decay_log,
    skip_gain,
    out_proj,
    router_gain,
    router,
    expert_up,
    expert_down,
):
    tokens_n = block_input.shape[0]
    kernel_taps = conv_weight.shape[0]
    inner_width = in_proj.shape[1] // 2
    low_rank = step_proj.shape[0]
    state_size = decay_log.shape[1]
    experts_n = router.shape[1]
    capacity = (5 * tokens_n + 4 * experts_n - 1) // (4 * experts_n)
    span_index = lax.axis_index(("seq", "exp"))
    span_first = span_index * tokens_n
    position = span_first + jnp.arange(tokens_n, dtype=jnp.int32)
    seq_starts = jnp.cumsum(seq_lengths) - seq_lengths
    before = seq_starts[None, :] <= position[:, None]
    own_start = jnp.max(jnp.where(before, seq_starts[None, :], 0), axis=1)
    fresh = (own_start == position).astype(jnp.float32)
    alive = (own_start < span_first).astype(jnp.float32)
    tap_pos = (
        position[:, None] - (kernel_taps - 1) + jnp.arange(kernel_taps, dtype=jnp.int32)[None, :]
    )
    tap_valid = (tap_pos >= own_start[:, None]).astype(jnp.float32)

    def project_in(block_input, mixer_gain, in_proj):
        joined = matmul_high(rms_scale(block_input, mixer_gain), in_proj)
        return (joined[:, :inner_width], joined[:, inner_width:])

    def conv_features(extended, conv_weight, conv_bias, state_proj, step_proj, step_bias):
        summed = jnp.broadcast_to(conv_bias[None, :], (tokens_n, inner_width))
        for offset in range(kernel_taps):
            summed = (
                summed
                + extended[offset : offset + tokens_n]
                * tap_valid[:, offset : offset + 1]
                * conv_weight[offset][None, :]
            )
        activated = jax.nn.silu(summed)
        projected = matmul_high(activated, state_proj)
        step_sizes = jax.nn.softplus(matmul_high(projected[:, :low_rank], step_proj) + step_bias)
        return (
            activated,
            step_sizes,
            projected[:, low_rank : low_rank + state_size],
            projected[:, low_rank + state_size :],
        )

    def scan_part(activated, step_sizes, in_state, out_state, decay_log):
        decay_rate = -jnp.exp(decay_log)
        block_len = min(32, tokens_n)
        blocks = tokens_n // block_len

        def advance(carried, pieces):
            act_b, step_b, in_b, out_b, fresh_b = pieces
            outputs = []
            for index in range(block_len):
                decay_now = jnp.exp(step_b[index][:, None] * decay_rate) * (1.0 - fresh_b[index])
                carried = (
                    decay_now * carried
                    + (step_b[index] * act_b[index])[:, None] * in_b[index][None, :]
                )
                outputs.append(jnp.sum(carried * out_b[index][None, :], axis=1))
            return (carried, jnp.stack(outputs))

        pieces = tuple(
            (
                member.reshape((blocks, block_len) + member.shape[1:])
                for member in (activated, step_sizes, in_state, out_state, fresh)
            )
        )
        zero_end, local_out = lax.scan(advance, jnp.zeros(decay_log.shape, jnp.float32), pieces)
        running_end = jnp.sum(step_sizes, axis=0)
        end_decay = jnp.exp(running_end[:, None] * decay_rate) * alive[tokens_n - 1]
        return (local_out.reshape(tokens_n, -1), zero_end, end_decay)

    def carry_terms(out_state, step_sizes, decay_log, start_state):
        decay_rate = -jnp.exp(decay_log)
        running = jnp.cumsum(step_sizes, axis=0)
        block_len = min(64, tokens_n)
        blocks = tokens_n // block_len

        def one_block(pieces):
            run_b, out_b, alive_b = pieces
            factor = jnp.exp(run_b[:, :, None] * decay_rate[None]) * start_state[None]
            return jnp.sum(factor * out_b[:, None, :], axis=2) * alive_b[:, None]

        shaped = (
            running.reshape(blocks, block_len, -1),
            out_state.reshape(blocks, block_len, -1),
            alive.reshape(blocks, block_len),
        )
        return lax.map(one_block, shaped).reshape(tokens_n, -1)

    def mixer_out(scan_out, activated, gate_z, skip_gain, out_proj, block_input):
        return block_input + matmul_high(
            (scan_out + skip_gain * activated) * jax.nn.silu(gate_z), out_proj
        )

    chosen = (expert_ids == jnp.arange(experts_n, dtype=jnp.int32)[None, :]).astype(jnp.float32)

    def route(resid, router_gain, router):
        normed_moe = rms_scale(resid, router_gain)
        probs = jax.nn.softmax(matmul_high(normed_moe, router), axis=1)
        return (normed_moe, jnp.sum(probs * chosen, axis=1))

    (inner_x, gate_z), proj_back = jax.vjp(project_in, block_input, mixer_gain, in_proj)
    previous = passed_along(inner_x[tokens_n - kernel_taps + 1 :], ("seq", "exp"), 1)
    extended = jnp.concatenate([previous, inner_x], axis=0)
    (activated, step_sizes, in_state, out_state), conv_back = jax.vjp(
        conv_features, extended, conv_weight, conv_bias, state_proj, step_proj, step_bias
    )
    (local_out, zero_end, end_decay), scan_back = jax.vjp(
        scan_part, activated, step_sizes, in_state, out_state, decay_log
    )
    identity_pair = (jnp.ones_like(end_decay), jnp.zeros_like(zero_end))
    start_state = entering(
        (end_decay, zero_end), ("seq", "exp"), chain_states, identity_pair, False
    )[1]
    correction, carry_back = jax.vjp(carry_terms, out_state, step_sizes, decay_log, start_state)
    scan_out = local_out + correction
    resid, mixer_back = jax.vjp(
        mixer_out, scan_out, activated, gate_z, skip_gain, out_proj, block_input
    )
    (normed_moe, gate), route_back = jax.vjp(route, resid, router_gain, router)
    ahead_count = jnp.cumsum(chosen, axis=0) - chosen
    slot_rank = jnp.sum(ahead_count * chosen, axis=1).astype(jnp.int32)
    kept = (slot_rank < capacity).astype(jnp.float32)
    slot_ids = expert_ids[:, 0] * capacity + slot_rank
    dispatch = (
        jnp.arange(experts_n * capacity, dtype=jnp.int32)[:, None] == slot_ids[None, :]
    ).astype(jnp.float32) * kept[None, :]
    buffer = matmul_high(dispatch, normed_moe).reshape(experts_n, capacity, -1)
    full_up, full_down = (
        lax.all_gather(expert_up, "seq", axis=2, tiled=True),
        lax.all_gather(expert_down, "seq", axis=1, tiled=True),
    )
    received = lax.all_to_all(buffer, "exp", split_axis=0, concat_axis=0, tiled=True)
    local_n = full_up.shape[0]
    items = received.shape[1]
    grouped = received.reshape(-1, local_n, items, received.shape[2])
    hidden_pre = jnp.einsum("secd,edf->secf", grouped, full_up, precision=precise)
    result = jnp.einsum("secf,efd->secd", jax.nn.gelu(hidden_pre), full_down, precision=precise)
    returned = lax.all_to_all(
        result.reshape(received.shape), "exp", split_axis=0, concat_axis=0, tiled=True
    )
    returned, received, hidden_pre = (
        returned,
        received,
        hidden_pre.reshape(received.shape[0], items, -1),
    )
    combined = jnp.einsum(
        "st,sd->td", dispatch, returned.reshape(experts_n * capacity, -1), precision=precise
    )
    block_output = resid + gate[:, None] * combined
    grad_gate = jnp.sum(output_grad * combined, axis=1)
    grad_back = jnp.einsum(
        "st,td->sd", dispatch, output_grad * gate[:, None], precision=precise
    ).reshape(experts_n, capacity, -1)
    grad_result = lax.all_to_all(grad_back, "exp", split_axis=0, concat_axis=0, tiled=True)
    use_up, use_down = (
        lax.all_gather(expert_up, "seq", axis=2, tiled=True),
        lax.all_gather(expert_down, "seq", axis=1, tiled=True),
    )
    local_n = use_up.shape[0]
    sources = grad_result.shape[0] // local_n
    grad_group = grad_result.reshape(sources, local_n, capacity, -1)
    hidden_group = hidden_pre.reshape(sources, local_n, capacity, -1)
    input_group = received.reshape(sources, local_n, capacity, -1)
    gelu_hidden, gelu_back = jax.vjp(jax.nn.gelu, hidden_group)
    grad_down_full = jnp.einsum("secf,secd->efd", gelu_hidden, grad_group, precision=precise)
    grad_hidden = gelu_back(jnp.einsum("secd,efd->secf", grad_group, use_down, precision=precise))[
        0
    ]
    grad_up_full = jnp.einsum("secd,secf->edf", input_group, grad_hidden, precision=precise)
    grad_received = jnp.einsum("secf,edf->secd", grad_hidden, use_up, precision=precise).reshape(
        grad_result.shape
    )
    grad_buffer = lax.all_to_all(grad_received, "exp", split_axis=0, concat_axis=0, tiled=True)
    grad_expert_up, grad_expert_down = (
        lax.psum_scatter(grad_up_full, "seq", scatter_dimension=2, tiled=True),
        lax.psum_scatter(grad_down_full, "seq", scatter_dimension=1, tiled=True),
    )
    grad_normed_moe = jnp.einsum(
        "st,sd->td", dispatch, grad_buffer.reshape(experts_n * capacity, -1), precision=precise
    )
    grad_resid_route, grad_router_gain, grad_router = route_back((grad_normed_moe, grad_gate))
    grad_resid = output_grad + grad_resid_route
    grad_scan, grad_act_mix, grad_gate_z, grad_skip_gain, grad_out_proj, grad_input_mix = (
        mixer_back(grad_resid)
    )
    grad_out_carry, grad_step_carry, grad_decay_carry, grad_start = carry_back(grad_scan)
    grad_end = entering((end_decay, grad_start), ("seq", "exp"), chain_states, identity_pair, True)[
        1
    ]
    grad_act_scan, grad_step_scan, grad_in_state, grad_out_scan, grad_decay_scan = scan_back(
        (grad_scan, grad_end, grad_end * start_state)
    )
    (
        grad_extended,
        grad_conv_weight,
        grad_conv_bias,
        grad_state_proj,
        grad_step_proj,
        grad_step_bias,
    ) = conv_back(
        (
            grad_act_mix + grad_act_scan,
            grad_step_carry + grad_step_scan,
            grad_in_state,
            grad_out_carry + grad_out_scan,
        )
    )
    edge_grad = passed_along(grad_extended[: kernel_taps - 1], ("seq", "exp"), -1)
    grad_inner = grad_extended[kernel_taps - 1 :] + jnp.concatenate(
        [jnp.zeros((tokens_n - kernel_taps + 1, inner_width), jnp.float32), edge_grad], axis=0
    )
    grad_input_proj, grad_mixer_gain, grad_in_proj = proj_back((grad_inner, grad_gate_z))
    input_grad = grad_input_mix + grad_input_proj
    grad_decay_log = grad_decay_carry + grad_decay_scan
    load_local = jnp.sum(chosen, axis=0)
    drop_local = jnp.sum(chosen * (1.0 - kept)[:, None], axis=0)
    summed_grads = lax.psum(
        (
            grad_mixer_gain,
            grad_in_proj,
            grad_conv_weight,
            grad_conv_bias,
            grad_state_proj,
            grad_step_proj,
            grad_step_bias,
            grad_decay_log,
            grad_skip_gain,
            grad_out_proj,
            grad_router_gain,
            grad_router,
            load_local,
            drop_local,
        ),
        ("seq", "exp"),
    )
    expert_load = summed_grads[12].astype(jnp.int32)
    dropped_load = summed_grads[13].astype(jnp.int32)
    return (
        block_output,
        input_grad,
        summed_grads[0],
        summed_grads[1],
        summed_grads[2],
        summed_grads[3],
        summed_grads[4],
        summed_grads[5],
        summed_grads[6],
        summed_grads[7],
        summed_grads[8],
        summed_grads[9],
        summed_grads[10],
        summed_grads[11],
        grad_expert_up,
        grad_expert_down,
        expert_load,
        dropped_load,
    )


def solution(mesh):
    in_specs = (
        P(("seq", "exp"), None),
        P(),
        P(("seq", "exp"), None),
        P(("seq", "exp"), None),
        P(),
        P(),
        P(),
        P(),
        P(),
        P(),
        P(),
        P(),
        P(),
        P(),
        P(),
        P(),
        P("exp", None, "seq"),
        P("exp", "seq", None),
    )
    out_specs = (
        P(("seq", "exp"), None),
        P(("seq", "exp"), None),
        P(),
        P(),
        P(),
        P(),
        P(),
        P(),
        P(),
        P(),
        P(),
        P(),
        P(),
        P(),
        P("exp", None, "seq"),
        P("exp", "seq", None),
        P(),
        P(),
    )
    return jax.shard_map(
        per_device, mesh=mesh, in_specs=in_specs, out_specs=out_specs, check_vma=False
    )
```

profile of v0, /device:TPU:0, one launch (start us, length us, event | category | flops | bytes accessed | tf_op | source)
XLA Modules:
  0.0 3072.7 jit_solution(16956716026353753182)
XLA Ops:
  9.0 7.8 fusion.626
  36.6 739.4 %while.750 = (s32[]{:T(128)}, f32[1536,16]{0,1:T(8,128)S(1)}, f32[4,32,1536]{2,1,0:T(8,128)}, f32[4,1536,1]{1,2,0:T(1,128)}, f32[4,1536,16]{1,2,0:T(8,128)}, /*i...) while((s32[]{:T(128)}, f32[1536,16]{0,1:T(8,128)S(1)}, ...), condition=%wide.region_36.37_spmd.clone, body=%wide.region_3.36_spmd.clone.sunk | while | flops 11132994 | bytes 24794744 | solution.py:135
  785.7 52.7 %all-gather.15.cloned.1.call-done = f32[49152,16]{0,1:T(8,128)} async-done(((f32[1536,16]{0,1:T(8,128)}), f32[49152,16]{0,1:T(8,128)}) %all-gather.15.cloned.1.call-update) | async-done | bytes 3145744 | tf_op jit(solution)/shard_map/all_gather | solution.py:18
  838.5 5.4 copy.107
  843.9 56.0 %all-gather.13.cloned.1.call-done = f32[49152,16]{0,1:T(8,128)} async-done(((f32[1536,16]{0,1:T(8,128)}), f32[49152,16]{0,1:T(8,128)}) %all-gather.13.cloned.1.call-update) | async-done | bytes 3145744 | tf_op jit(solution)/shard_map/all_gather | solution.py:18
  903.7 68.8 %while.751 = (s32[]{:T(128)}, f32[1536,16]{0,1:T(8,128)S(1)}, s32[]{:T(128)}, f32[32,1536,16]{1,2,0:T(8,128)}, f32[32,1536,16]{1,0,2:T(8,128)}, /*index=5*/s32[]{:T(128)}, s32[]{:T(128)}) while((s32[]{:T(128)}, f32[1536,16]{0,1:T(8,128)S(1)}, s32[]{:T(128)}, f32[32,1536,16]{1,2,0:T(8,128)}, f32[32,1536,16]{1,0,2:T(8,128)}, ...), condition=%wide.region_40.41_spmd.clone, body=%wide.region_39.40_spmd.clone.sunk | while | flops 98308 | bytes 589929 | solution.py:30
  973.4 25.3 while.749
  978.1 6.1 multiply_dynamic-update-slice_fusion.38
  990.7 6.3 multiply_dynamic-update-slice_fusion.38
  1000.8 5.6 multiply_reduce_fusion.141
  1012.8 7.9 all-to-all-done
  1021.5 17.0 all-gather.9.cloned.1.call-done
  1038.5 8.4 fusion.586
  1046.9 129.9 %all-gather.11.cloned.1.call-done = f32[1,3072,768]{2,1,0:T(8,128)} async-done(((f32[1,384,768]{2,1,0:T(8,128)}), f32[1,3072,768]{2,1,0:T(8,128)}) %all-gather.11.cloned.1.call-update) | async-done | bytes 9437200 | tf_op jit(solution)/shard_map/all_gather | solution.py:199
  1176.8 9.3 fusion.580
  1192.9 5.9 all-to-all-done.1
  1204.4 11.1 all_to_all.20
  1215.5 13.0 fusion.598
  1229.9 13.1 fusion.582
  1247.7 7.3 all-to-all-done.3
  1258.2 9.3 multiply_reduce_fusion.131
  1269.1 23.9 while.752
  1271.6 7.2 multiply_reduce_fusion.199
  1283.5 7.2 multiply_reduce_fusion.199
  1299.4 15.4 reduce_window_sum.42
  1314.8 7.2 fusion.700
  1322.1 28.1 all-gather.17.cloned.1.call-done
  1350.2 5.4 copy.108
  1355.6 8.1 rev.7
  1363.7 68.2 %while.753 = (s32[]{:T(128)}, f32[1536,16]{0,1:T(8,128)S(1)}, s32[]{:T(128)}, f32[32,1536,16]{1,2,0:T(8,128)}, f32[32,1536,16]{1,0,2:T(8,128)}, /*index=5*/s32[]{:T(128)}, s32[]{:T(128)}) while((s32[]{:T(128)}, f32[1536,16]{0,1:T(8,128)S(1)}, s32[]{:T(128)}, f32[32,1536,16]{1,2,0:T(8,128)}, f32[32,1536,16]{1,0,2:T(8,128)}, ...), condition=%wide.region_60.61_spmd.clone, body=%wide.region_59.60_spmd.clone.sunk | while | flops 98308 | bytes 589929 | solution.py:30
  1435.2 710.6 %while.754 = (s32[]{:T(128)}, f32[1536,16]{0,1:T(8,128)}, f32[1536,16]{0,1:T(8,128)S(1)}, f32[4,32,1536]{2,1,0:T(8,128)}, f32[4,32,1536]{2,1,0:T(8,128)}, /*inde...) while((s32[]{:T(128)}, f32[1536,16]{0,1:T(8,128)}, ...), condition=%wide.region_190.191_spmd.clone, body=%wide.region_61.190_spmd.clone.sunk | while | flops 17356836 | bytes 57770112 | solution.py:135
  1464.6 13.3 multiply_reduce_fusion.200
  1507.0 15.2 multiply_reduce_fusion.201
  1642.2 13.3 multiply_reduce_fusion.200
  1684.4 15.2 multiply_reduce_fusion.201
  1819.7 13.3 multiply_reduce_fusion.200
  1862.1 15.2 multiply_reduce_fusion.201
  1996.8 13.3 multiply_reduce_fusion.200
  2039.2 15.2 multiply_reduce_fusion.201
  2160.5 10.1 fusion.603
  2172.2 10.4 convolution_bitcast_fusion
  2184.4 10.3 convolution_bitcast_fusion.1
  2196.3 12.1 multiply_reduce_fusion.137
  2208.5 44.7 %all-reduce.174 = (f32[768]{0:T(1024)}, f32[4,1536]{1,0:T(4,128)}, f32[1536]{0:T(1024)}, f32[1536]{0:T(1024)}, f32[1536]{0:T(1024)}, /*index=5*/f32[768]{0:T(102...) all-reduce(f32[768]{0:T(1024)S(1)} %get-tuple-element.12840, ...), channel_id=1, replica_groups=mesh['seq'=8,'exp'=4] {'seq','exp'}, use_global_device_ids=true, to_apply=%region_195.196 | all-reduce | flops 15368 | bytes 122944 | tf_op jit(solution)/shard_map/psum | solution.py:286
  2255.1 459.9 %all-reduce.178.cloned.1.call-done = (f32[768,3072]{1,0:T(8,128)}, f32[1536,80]{0,1:T(8,128)}, f32[48,1536]{1,0:T(8,128)}, f32[1536,16]{0,1:T(8,128)}, f32[1536,768]{1,0:T(8,128)}) async-done(((f32[768,3072]{1,0:T(8,128)}, f32[1536,80]{0,1:T(8,128)}, f32[48,1536]{1,0:T(8,128)}, f32[1536,16]{0,1:T(8,128)}, f32[1536,768]{1,0:T(8,128)}), (f32[768,3072]{1,0:T(8,128)}, f32[1536,80]{0,1:T(8,128)}, ...) | async-done | bytes 15040528 | tf_op jit(solution)/shard_map/psum | solution.py:286
  2715.1 170.9 %reduce-scatter.5.cloned.1.call-done = f32[1,384,768]{2,1,0:T(8,128)} async-done(((f32[1,3072,768]{2,1,0:T(8,128)}), f32[1,384,768]{2,1,0:T(8,128)}) %reduce-scatter.5.cloned.1.call-update) | async-done | bytes 1179664 | tf_op jit(solution)/shard_map/reduce_scatter | solution.py:245
  2885.9 166.6 %reduce-scatter.3.cloned.1.call-done = f32[1,768,384]{2,1,0:T(8,128)} async-done(((f32[1,768,3072]{2,1,0:T(8,128)}), f32[1,768,384]{2,1,0:T(8,128)}) %reduce-scatter.3.cloned.1.call-update) | async-done | bytes 1179664 | tf_op jit(solution)/shard_map/reduce_scatter | solution.py:244
  3052.5 8.8 copy.1512
  (3618 shorter events, 1503.1 us)
Async XLA Ops:
  7.2 831.3 %all-gather.15.cloned.1.call-start = ((), (), s32[]{:S(2)}) async-start(), calls=%async_computation.11 | async-start | bytes 3244032 | tf_op jit(solution)/shard_map/all_gather | solution.py:18
  16.8 9.4 collective-permute-start
  113.4 108.3 %copy-start.100 = (f32[4,32,16]{2,1,0:T(8,128)S(1)}, f32[4,32,16]{2,1,0:T(8,128)}, u32[]{:S(2)}) copy-start(f32[4,32,16]{2,1,0:T(8,128)} %copy-done.99) | copy-start | bytes 24580 | tf_op jit(solution)/shard_map/jvp()/while
  113.4 108.3 %copy-start.192 = (f32[4,1,16]{2,1,0:T(1,128)S(1)}, f32[4,1,16]{2,1,0:T(1,128)}, u32[]{:S(2)}) copy-start(f32[4,1,16]{2,1,0:T(1,128)} %copy-done.191) | copy-start | bytes 772 | tf_op jit(solution)/shard_map/jvp()/while
  117.0 104.5 %copy-start.205 = (f32[4]{0:T(128)}, f32[4]{0:T(128)S(1)}, u32[]{:S(2)}) copy-start(f32[4]{0:T(128)S(1)} %get-tuple-element.21621) | copy-start | bytes 52 | tf_op jit(solution)/shard_map/jvp()/while
  117.0 104.5 %copy-start.221 = (f32[4]{0:T(128)}, f32[4]{0:T(128)S(1)}, u32[]{:S(2)}) copy-start(f32[4]{0:T(128)S(1)} %get-tuple-element.21632) | copy-start | bytes 52 | tf_op jit(solution)/shard_map/jvp()/while
  117.1 104.4 %copy-start.225 = (f32[4]{0:T(128)}, f32[4]{0:T(128)S(1)}, u32[]{:S(2)}) copy-start(f32[4]{0:T(128)S(1)} %get-tuple-element.21642) | copy-start | bytes 52 | tf_op jit(solution)/shard_map/jvp()/while
  117.1 104.4 %copy-start.227 = (f32[4]{0:T(128)}, f32[4]{0:T(128)S(1)}, u32[]{:S(2)}) copy-start(f32[4]{0:T(128)S(1)} %get-tuple-element.21652) | copy-start | bytes 52 | tf_op jit(solution)/shard_map/jvp()/while
  117.2 104.4 %copy-start.229 = (f32[4]{0:T(128)}, f32[4]{0:T(128)S(1)}, u32[]{:S(2)}) copy-start(f32[4]{0:T(128)S(1)} %get-tuple-element.21662) | copy-start | bytes 52 | tf_op jit(solution)/shard_map/jvp()/while
  117.2 104.4 %copy-start.231 = (f32[4]{0:T(128)}, f32[4]{0:T(128)S(1)}, u32[]{:S(2)}) copy-start(f32[4]{0:T(128)S(1)} %get-tuple-element.21672) | copy-start | bytes 52 | tf_op jit(solution)/shard_map/jvp()/while
  298.1 108.3 %copy-start.100 = (f32[4,32,16]{2,1,0:T(8,128)S(1)}, f32[4,32,16]{2,1,0:T(8,128)}, u32[]{:S(2)}) copy-start(f32[4,32,16]{2,1,0:T(8,128)} %copy-done.99) | copy-start | bytes 24580 | tf_op jit(solution)/shard_map/jvp()/while
  298.1 108.3 %copy-start.192 = (f32[4,1,16]{2,1,0:T(1,128)S(1)}, f32[4,1,16]{2,1,0:T(1,128)}, u32[]{:S(2)}) copy-start(f32[4,1,16]{2,1,0:T(1,128)} %copy-done.191) | copy-start | bytes 772 | tf_op jit(solution)/shard_map/jvp()/while
  301.7 104.5 %copy-start.205 = (f32[4]{0:T(128)}, f32[4]{0:T(128)S(1)}, u32[]{:S(2)}) copy-start(f32[4]{0:T(128)S(1)} %get-tuple-element.21621) | copy-start | bytes 52 | tf_op jit(solution)/shard_map/jvp()/while
  301.7 104.5 %copy-start.221 = (f32[4]{0:T(128)}, f32[4]{0:T(128)S(1)}, u32[]{:S(2)}) copy-start(f32[4]{0:T(128)S(1)} %get-tuple-element.21632) | copy-start | bytes 52 | tf_op jit(solution)/shard_map/jvp()/while
  301.8 104.4 %copy-start.225 = (f32[4]{0:T(128)}, f32[4]{0:T(128)S(1)}, u32[]{:S(2)}) copy-start(f32[4]{0:T(128)S(1)} %get-tuple-element.21642) | copy-start | bytes 52 | tf_op jit(solution)/shard_map/jvp()/while
  301.8 104.4 %copy-start.227 = (f32[4]{0:T(128)}, f32[4]{0:T(128)S(1)}, u32[]{:S(2)}) copy-start(f32[4]{0:T(128)S(1)} %get-tuple-element.21652) | copy-start | bytes 52 | tf_op jit(solution)/shard_map/jvp()/while
  301.9 104.4 %copy-start.229 = (f32[4]{0:T(128)}, f32[4]{0:T(128)S(1)}, u32[]{:S(2)}) copy-start(f32[4]{0:T(128)S(1)} %get-tuple-element.21662) | copy-start | bytes 52 | tf_op jit(solution)/shard_map/jvp()/while
  301.9 104.4 %copy-start.231 = (f32[4]{0:T(128)}, f32[4]{0:T(128)S(1)}, u32[]{:S(2)}) copy-start(f32[4]{0:T(128)S(1)} %get-tuple-element.21672) | copy-start | bytes 52 | tf_op jit(solution)/shard_map/jvp()/while
  482.7 108.4 %copy-start.100 = (f32[4,32,16]{2,1,0:T(8,128)S(1)}, f32[4,32,16]{2,1,0:T(8,128)}, u32[]{:S(2)}) copy-start(f32[4,32,16]{2,1,0:T(8,128)} %copy-done.99) | copy-start | bytes 24580 | tf_op jit(solution)/shard_map/jvp()/while
  482.7 108.3 %copy-start.192 = (f32[4,1,16]{2,1,0:T(1,128)S(1)}, f32[4,1,16]{2,1,0:T(1,128)}, u32[]{:S(2)}) copy-start(f32[4,1,16]{2,1,0:T(1,128)} %copy-done.191) | copy-start | bytes 772 | tf_op jit(solution)/shard_map/jvp()/while
  486.3 104.6 %copy-start.205 = (f32[4]{0:T(128)}, f32[4]{0:T(128)S(1)}, u32[]{:S(2)}) copy-start(f32[4]{0:T(128)S(1)} %get-tuple-element.21621) | copy-start | bytes 52 | tf_op jit(solution)/shard_map/jvp()/while
  486.3 104.6 %copy-start.221 = (f32[4]{0:T(128)}, f32[4]{0:T(128)S(1)}, u32[]{:S(2)}) copy-start(f32[4]{0:T(128)S(1)} %get-tuple-element.21632) | copy-start | bytes 52 | tf_op jit(solution)/shard_map/jvp()/while
  486.4 104.5 %copy-start.225 = (f32[4]{0:T(128)}, f32[4]{0:T(128)S(1)}, u32[]{:S(2)}) copy-start(f32[4]{0:T(128)S(1)} %get-tuple-element.21642) | copy-start | bytes 52 | tf_op jit(solution)/shard_map/jvp()/while
  486.4 104.5 %copy-start.227 = (f32[4]{0:T(128)}, f32[4]{0:T(128)S(1)}, u32[]{:S(2)}) copy-start(f32[4]{0:T(128)S(1)} %get-tuple-element.21652) | copy-start | bytes 52 | tf_op jit(solution)/shard_map/jvp()/while
  486.5 104.4 %copy-start.229 = (f32[4]{0:T(128)}, f32[4]{0:T(128)S(1)}, u32[]{:S(2)}) copy-start(f32[4]{0:T(128)S(1)} %get-tuple-element.21662) | copy-start | bytes 52 | tf_op jit(solution)/shard_map/jvp()/while
  486.5 104.4 %copy-start.231 = (f32[4]{0:T(128)}, f32[4]{0:T(128)S(1)}, u32[]{:S(2)}) copy-start(f32[4]{0:T(128)S(1)} %get-tuple-element.21672) | copy-start | bytes 52 | tf_op jit(solution)/shard_map/jvp()/while
  486.6 104.3 %copy-start.233 = (f32[4]{0:T(128)}, f32[4]{0:T(128)S(1)}, u32[]{:S(2)}) copy-start(f32[4]{0:T(128)S(1)} %get-tuple-element.21682) | copy-start | bytes 52 | tf_op jit(solution)/shard_map/jvp()/while
  667.5 108.3 %copy-start.100 = (f32[4,32,16]{2,1,0:T(8,128)S(1)}, f32[4,32,16]{2,1,0:T(8,128)}, u32[]{:S(2)}) copy-start(f32[4,32,16]{2,1,0:T(8,128)} %copy-done.99) | copy-start | bytes 24580 | tf_op jit(solution)/shard_map/jvp()/while
  667.5 108.3 %copy-start.192 = (f32[4,1,16]{2,1,0:T(1,128)S(1)}, f32[4,1,16]{2,1,0:T(1,128)}, u32[]{:S(2)}) copy-start(f32[4,1,16]{2,1,0:T(1,128)} %copy-done.191) | copy-start | bytes 772 | tf_op jit(solution)/shard_map/jvp()/while
  671.1 104.5 %copy-start.205 = (f32[4]{0:T(128)}, f32[4]{0:T(128)S(1)}, u32[]{:S(2)}) copy-start(f32[4]{0:T(128)S(1)} %get-tuple-element.21621) | copy-start | bytes 52 | tf_op jit(solution)/shard_map/jvp()/while
  671.1 104.5 %copy-start.221 = (f32[4]{0:T(128)}, f32[4]{0:T(128)S(1)}, u32[]{:S(2)}) copy-start(f32[4]{0:T(128)S(1)} %get-tuple-element.21632) | copy-start | bytes 52 | tf_op jit(solution)/shard_map/jvp()/while
  671.2 104.4 %copy-start.225 = (f32[4]{0:T(128)}, f32[4]{0:T(128)S(1)}, u32[]{:S(2)}) copy-start(f32[4]{0:T(128)S(1)} %get-tuple-element.21642) | copy-start | bytes 52 | tf_op jit(solution)/shard_map/jvp()/while
  671.2 104.4 %copy-start.227 = (f32[4]{0:T(128)}, f32[4]{0:T(128)S(1)}, u32[]{:S(2)}) copy-start(f32[4]{0:T(128)S(1)} %get-tuple-element.21652) | copy-start | bytes 52 | tf_op jit(solution)/shard_map/jvp()/while
  671.3 104.4 %copy-start.229 = (f32[4]{0:T(128)}, f32[4]{0:T(128)S(1)}, u32[]{:S(2)}) copy-start(f32[4]{0:T(128)S(1)} %get-tuple-element.21662) | copy-start | bytes 52 | tf_op jit(solution)/shard_map/jvp()/while
  671.3 104.4 %copy-start.231 = (f32[4]{0:T(128)}, f32[4]{0:T(128)S(1)}, u32[]{:S(2)}) copy-start(f32[4]{0:T(128)S(1)} %get-tuple-element.21672) | copy-start | bytes 52 | tf_op jit(solution)/shard_map/jvp()/while
  776.7 123.1 %all-gather.13.cloned.1.call-start = ((), (), s32[]{:S(2)}) async-start(), calls=%async_computation.10 | async-start | bytes 3244032 | tf_op jit(solution)/shard_map/all_gather | solution.py:18
  777.4 261.1 %all-gather.9.cloned.1.call-start = ((), (), s32[]{:S(2)}) async-start(), calls=%async_computation.6 | async-start | bytes 10616832 | tf_op jit(solution)/shard_map/all_gather | solution.py:198
  778.2 398.6 %all-gather.11.cloned.1.call-start = ((), (), s32[]{:S(2)}) async-start(), calls=%async_computation.7 | async-start | bytes 10616832 | tf_op jit(solution)/shard_map/all_gather | solution.py:199
  1006.4 249.8 %copy-start.150 = (f32[128]{0:T(128)}, f32[128]{0:T(128)S(1)}, u32[]{:S(2)}) copy-start(f32[128]{0:T(128)S(1)} %fusion.679) | copy-start | bytes 1540
  1008.6 12.1 all-to-all-start
  1046.9 168.6 %copy-start.2 = (f32[4,1,40,3072]{3,2,0,1:T(8,128)}, f32[4,1,40,3072]{3,2,0,1:T(8,128)S(1)}, u32[]{:S(2)}) copy-start(f32[4,1,40,3072]{3,2,0,1:T(8,128)S(1)} %fusion.586) | copy-start | bytes 5898244
  1186.1 12.7 all-to-all-start.1
  1243.0 12.1 all-to-all-start.3
  1246.6 103.6 %all-gather.17.cloned.1.call-start = ((), (), s32[]{:S(2)}) async-start(), calls=%async_computation.12 | async-start | bytes 3244032 | tf_op jit(solution)/shard_map/all_gather | solution.py:18
  1293.7 1421.4 %all-reduce.178.cloned.1.call-start = ((), (), s32[]{:S(2)}) async-start(), calls=%async_computation.13 | async-start | bytes 30081024 | tf_op jit(solution)/shard_map/psum | solution.py:286
  2157.3 3.1 collective-permute-start.1
  2170.6 715.3 %reduce-scatter.5.cloned.1.call-start = ((), (), s32[]{:S(2)}) async-start(), calls=%async_computation.9 | async-start | bytes 10616832 | tf_op jit(solution)/shard_map/reduce_scatter | solution.py:245
  2182.7 869.9 %reduce-scatter.3.cloned.1.call-start = ((), (), s32[]{:S(2)}) async-start(), calls=%async_computation.8 | async-start | bytes 10616832 | tf_op jit(solution)/shard_map/reduce_scatter | solution.py:244
  (580 other events, 15909.9 us)
Sparse Core Ops, SparseCore 0:
  776.8 61.6 all-gather.14
  842.0 57.7 all-gather.12
  902.0 136.5 all-gather.8
  1040.6 136.1 all-gather.10
  1293.8 56.3 all-gather.16
  2170.8 544.2 all-reduce.177
  2721.2 164.7 reduce-scatter.4
  2890.1 162.3 reduce-scatter.2
where the time goes:
time: 3120 us; the launch traced here: 3070 us
  local copies, waits for them, and re-layouts  1110 us (36%)
  waiting for transfers between devices  1100 us (35%)
  other arithmetic  544 us (17%)
  matrix products  135 us (4%)
  loops' own time  92.2 us (3%)
  blocking collectives  55.8 us (2%)
    psum x1, waiting for transfers between devices, per_device(): lax.psum((grad_mixer_gain, grad_in_proj, grad_conv_weight, grad_conv_bias...  460 us
    dynamic_update_slice x388, local copies, waits for them, and re-layouts, scan_part(): lax.scan(advance, jnp.zeros(decay_log.shape, jnp.float32), pieces)  453 us
    dynamic_slice x324, local copies, waits for them, and re-layouts, scan_part(): lax.scan(advance, jnp.zeros(decay_log.shape, jnp.float32), pieces)  285 us
    reduce_scatter x1, waiting for transfers between devices, per_device(): lax.psum_scatter(grad_down_full, 'seq', scatter_dimension=1, tiled=True)  171 us
    reduce_scatter x1, waiting for transfers between devices, per_device(): lax.psum_scatter(grad_up_full, 'seq', scatter_dimension=2, tiled=True)  167 us
    all_gather x3, waiting for transfers between devices, entering(): pieces = jax.tree.map(lambda part: lax.all_gather(part, axis), value)  137 us
    all_gather x1, waiting for transfers between devices, per_device(): lax.all_gather(expert_down, 'seq', axis=1, tiled=True)  130 us
    mul x196, other arithmetic, advance(): step_b[index] * act_b[index]  128 us
  transfers between devices with their start and end apart: 13, of which 12 were waited for; matrix products, arithmetic and copies ran while one was open for 6% of the time, Pallas kernels for 0%

commit v1 on v0

--- a/solution.py
+++ b/solution.py
@@ -5,6 +5,28 @@
 
 precise = lax.Precision.HIGHEST
 epsilon = 1e-05
+
+
+def in_order(blocks, dim):
+    blocks = jnp.moveaxis(blocks, 0, dim)
+    dims = blocks.shape
+    return blocks.reshape(*dims[:dim], dims[dim] * dims[dim + 1], *dims[dim + 2 :])
+
+
+def gather_around(x, axis, dim):
+    length = lax.axis_size(axis)
+    pairs = [(i, (i + 1) % length) for i in range(length)]
+    back = [(b, a) for a, b in pairs]
+    lower, upper = ([], [])
+    for lap in range(length - 1):
+        if lap % 2 == 0:
+            lower.append(lax.ppermute(lower[-1] if lower else x, axis, pairs))
+        else:
+            upper.append(lax.ppermute(upper[-1] if upper else x, axis, back))
+    parts = jnp.stack([*lower[::-1], x, *upper])
+    shift = lax.axis_index(axis) - len(lower)
+    parts = parts[(jnp.arange(length) - shift) % length]
+    return in_order(parts, dim)
 
 
 def passed_along(block, axis, distance):
@@ -196,7 +218,7 @@
     buffer = matmul_high(dispatch, normed_moe).reshape(experts_n, capacity, -1)
     full_up, full_down = (
         lax.all_gather(expert_up, "seq", axis=2, tiled=True),
-        lax.all_gather(expert_down, "seq", axis=1, tiled=True),
+        gather_around(expert_down, "seq", 1),
     )
     received = lax.all_to_all(buffer, "exp", split_axis=0, concat_axis=0, tiled=True)
     local_n = full_up.shape[0]

time: 3120 us -> 3170 us (1.016)
    ppermute x0 -> x7, waiting for transfers between devices: none -> 180 us  [the longest x4 180 us: gather_around(): lower.append(lax.ppermute(lower[-1] if lower else x, axis, pairs))]
    all_gather x3, waiting for transfers between devices: 137 us -> 28.1 us  [entering(): pieces = jax.tree.map(lambda part: lax.all_gather(part, axis), value)]
    all_gather x1, waiting for transfers between devices: 130 us -> 92.7 us  [per_device(): lax.all_gather(expert_down, 'seq', axis=1, tiled=True)]
  transfers between devices with their start and end apart: 13 -> 21, of which waited for: 12 -> 12; matrix products, arithmetic and copies ran while one was open for 6% -> 8% of each run, Pallas kernels for 0% -> 0%
where the time goes in v1:
time: 3170 us; the launch traced here: 3120 us
  local copies, waits for them, and re-layouts  1130 us (36%)
  waiting for transfers between devices  1110 us (35%)
  other arithmetic  543 us (17%)
  matrix products  135 us (4%)
  loops' own time  95.1 us (3%)
  blocking collectives  44.7 us (1%)
  starting transfers between devices  38.4 us (1%)
    psum x1, waiting for transfers between devices, per_device(): lax.psum((grad_mixer_gain, grad_in_proj, grad_conv_weight, grad_conv_bias...  459 us
    dynamic_update_slice x388, local copies, waits for them, and re-layouts, scan_part(): lax.scan(advance, jnp.zeros(decay_log.shape, jnp.float32), pieces)  451 us
    dynamic_slice x324, local copies, waits for them, and re-layouts, scan_part(): lax.scan(advance, jnp.zeros(decay_log.shape, jnp.float32), pieces)  283 us
    ppermute x4, waiting for transfers between devices, gather_around(): lower.append(lax.ppermute(lower[-1] if lower else x, axis, pairs))  180 us
    reduce_scatter x1, waiting for transfers between devices, per_device(): lax.psum_scatter(grad_down_full, 'seq', scatter_dimension=1, tiled=True)  171 us
    reduce_scatter x1, waiting for transfers between devices, per_device(): lax.psum_scatter(grad_up_full, 'seq', scatter_dimension=2, tiled=True)  167 us
    mul x196, other arithmetic, advance(): step_b[index] * act_b[index]  128 us
    reduce_sum x8, other arithmetic, advance(): step_b[index][:, None] * decay_rate  111 us
  transfers between devices with their start and end apart: 21, of which 12 were waited for; matrix products, arithmetic and copies ran while one was open for 8% of the time, Pallas kernels for 0%

profile of v1, /device:TPU:0, one launch (start us, length us, event | category | flops | bytes accessed | tf_op | source)
XLA Modules:
  0.0 3120.2 jit_solution(6525605452506020187)
XLA Ops:
  9.0 7.8 fusion.628
  36.6 740.7 %while.750 = (s32[]{:T(128)}, f32[1536,16]{0,1:T(8,128)S(1)}, f32[4,32,1536]{2,1,0:T(8,128)}, f32[4,1536,1]{1,2,0:T(1,128)}, f32[4,1536,16]{1,2,0:T(8,128)}, /*i...) while((s32[]{:T(128)}, f32[1536,16]{0,1:T(8,128)S(1)}, ...), condition=%wide.region_36.37_spmd.clone, body=%wide.region_3.36_spmd.clone.sunk | while | flops 11132994 | bytes 24794744 | solution.py:157
  782.1 31.3 %collective-permute-done.1 = f32[1,384,768]{2,1,0:T(8,128)S(1)} collective-permute-done((f32[1,384,768]{2,1,0:T(8,128)}, f32[1,384,768]{2,1,0:T(8,128)S(1)}, u32[]{:S(2)}, u32[]{:S(2)}) %collective-permute-start.1) | collective-permute-done | bytes 1179680 | tf_op jit(solution)/shard_map/ppermute | solution.py:23
  819.1 55.3 %collective-permute-done.2 = f32[1,384,768]{2,1,0:T(8,128)S(1)} collective-permute-done((f32[1,384,768]{2,1,0:T(8,128)S(1)}, f32[1,384,768]{2,1,0:T(8,128)S(1)}, u32[]{:S(2)}, u32[]{:S(2)}) %collective-permute-start.2) | collective-permute-done | bytes 1179680 | tf_op jit(solution)/shard_map/ppermute | solution.py:23
  880.4 50.7 %collective-permute-done.3 = f32[1,384,768]{2,1,0:T(8,128)} collective-permute-done((f32[1,384,768]{2,1,0:T(8,128)S(1)}, f32[1,384,768]{2,1,0:T(8,128)}, u32[]{:S(2)}, u32[]{:S(2)}) %collective-permute-start.3) | collective-permute-done | bytes 1179680 | tf_op jit(solution)/shard_map/ppermute | solution.py:23
  946.6 43.0 %collective-permute-done.4 = f32[1,384,768]{2,1,0:T(8,128)} collective-permute-done((f32[1,384,768]{2,1,0:T(8,128)}, f32[1,384,768]{2,1,0:T(8,128)}, u32[]{:S(2)}, u32[]{:S(2)}) %collective-permute-start.4) | collective-permute-done | bytes 1179680 | tf_op jit(solution)/shard_map/ppermute | solution.py:23
  1000.1 5.3 copy.107
  1009.3 68.6 %while.751 = (s32[]{:T(128)}, f32[1536,16]{0,1:T(8,128)S(1)}, s32[]{:T(128)}, f32[32,1536,16]{1,2,0:T(8,128)}, f32[32,1536,16]{1,0,2:T(8,128)}, /*index=5*/s32[]{:T(128)}, s32[]{:T(128)}) while((s32[]{:T(128)}, f32[1536,16]{0,1:T(8,128)S(1)}, s32[]{:T(128)}, f32[32,1536,16]{1,2,0:T(8,128)}, f32[32,1536,16]{1,0,2:T(8,128)}, ...), condition=%wide.region_40.41_spmd.clone, body=%wide.region_39.40_spmd.clone.sunk | while | flops 98308 | bytes 589929 | solution.py:52
  1078.9 25.3 while.749
  1083.6 6.1 multiply_dynamic-update-slice_fusion.38
  1096.2 6.3 multiply_dynamic-update-slice_fusion.38
  1106.3 5.6 multiply_reduce_fusion.141
  1122.4 8.6 gather_fusion
  1131.8 8.7 fusion.584
  1140.6 7.5 fusion.604
  1155.1 6.0 all-to-all-done.1
  1172.5 92.7 %all-gather.11.cloned.1.call-done = f32[1,3072,768]{2,1,0:T(8,128)} async-done(((f32[1,384,768]{2,1,0:T(8,128)}), f32[1,3072,768]{2,1,0:T(8,128)}) %all-gather.11.cloned.1.call-update) | async-done | bytes 9437200 | tf_op jit(solution)/shard_map/all_gather | solution.py:248
  1265.2 12.9 fusion.596
  1279.4 13.1 fusion.580
  1297.3 7.3 all-to-all-done.3
  1307.8 9.3 multiply_reduce_fusion.131
  1318.7 23.9 while.752
  1321.2 7.2 multiply_reduce_fusion.199
  1333.1 7.2 multiply_reduce_fusion.199
  1349.0 15.4 reduce_window_sum.42
  1364.5 7.2 fusion.704
  1371.7 28.1 all-gather.17.cloned.1.call-done
  1399.8 5.4 copy.108
  1405.2 8.1 rev.7
  1413.3 68.2 %while.753 = (s32[]{:T(128)}, f32[1536,16]{0,1:T(8,128)S(1)}, s32[]{:T(128)}, f32[32,1536,16]{1,2,0:T(8,128)}, f32[32,1536,16]{1,0,2:T(8,128)}, /*index=5*/s32[]{:T(128)}, s32[]{:T(128)}) while((s32[]{:T(128)}, f32[1536,16]{0,1:T(8,128)S(1)}, s32[]{:T(128)}, f32[32,1536,16]{1,2,0:T(8,128)}, f32[32,1536,16]{1,0,2:T(8,128)}, ...), condition=%wide.region_60.61_spmd.clone, body=%wide.region_59.60_spmd.clone.sunk | while | flops 98308 | bytes 589929 | solution.py:52
  1484.8 708.3 %while.754 = (s32[]{:T(128)}, f32[1536,16]{0,1:T(8,128)}, f32[1536,16]{0,1:T(8,128)S(1)}, f32[4,32,1536]{2,1,0:T(8,128)}, f32[4,32,1536]{2,1,0:T(8,128)}, /*inde...) while((s32[]{:T(128)}, f32[1536,16]{0,1:T(8,128)}, ...), condition=%wide.region_190.191_spmd.clone, body=%wide.region_61.190_spmd.clone.sunk | while | flops 17356836 | bytes 57770112 | solution.py:157
  1513.4 12.8 multiply_reduce_fusion.200
  1555.6 15.0 multiply_reduce_fusion.201
  1690.2 12.8 multiply_reduce_fusion.200
  1732.4 15.0 multiply_reduce_fusion.201
  1867.1 12.8 multiply_reduce_fusion.200
  1909.4 15.0 multiply_reduce_fusion.201
  2044.2 12.8 multiply_reduce_fusion.200
  2086.4 15.0 multiply_reduce_fusion.201
  2207.7 10.1 fusion.602
  2219.4 11.4 convolution_bitcast_fusion
  2232.4 10.3 convolution_bitcast_fusion.1
  2244.3 12.1 multiply_reduce_fusion.137
  2256.5 44.7 %all-reduce.174 = (f32[768]{0:T(1024)}, f32[4,1536]{1,0:T(4,128)}, f32[1536]{0:T(1024)}, f32[1536]{0:T(1024)}, f32[1536]{0:T(1024)}, /*index=5*/f32[768]{0:T(102...) all-reduce(f32[768]{0:T(1024)S(1)} %get-tuple-element.12840, ...), channel_id=1, replica_groups=mesh['seq'=8,'exp'=4] {'seq','exp'}, use_global_device_ids=true, to_apply=%region_195.196 | all-reduce | flops 15368 | bytes 122944 | tf_op jit(solution)/shard_map/psum | solution.py:308
  2303.2 459.4 %all-reduce.178.cloned.1.call-done = (f32[768,3072]{1,0:T(8,128)}, f32[1536,80]{0,1:T(8,128)}, f32[48,1536]{1,0:T(8,128)}, f32[1536,16]{0,1:T(8,128)}, f32[1536,768]{1,0:T(8,128)}) async-done(((f32[768,3072]{1,0:T(8,128)}, f32[1536,80]{0,1:T(8,128)}, f32[48,1536]{1,0:T(8,128)}, f32[1536,16]{0,1:T(8,128)}, f32[1536,768]{1,0:T(8,128)}), (f32[768,3072]{1,0:T(8,128)}, f32[1536,80]{0,1:T(8,128)}, ...) | async-done | bytes 15040528 | tf_op jit(solution)/shard_map/psum | solution.py:308
  2762.6 170.9 %reduce-scatter.5.cloned.1.call-done = f32[1,384,768]{2,1,0:T(8,128)} async-done(((f32[1,3072,768]{2,1,0:T(8,128)}), f32[1,384,768]{2,1,0:T(8,128)}) %reduce-scatter.5.cloned.1.call-update) | async-done | bytes 1179664 | tf_op jit(solution)/shard_map/reduce_scatter | solution.py:267
  2933.4 166.6 %reduce-scatter.3.cloned.1.call-done = f32[1,768,384]{2,1,0:T(8,128)} async-done(((f32[1,768,3072]{2,1,0:T(8,128)}), f32[1,768,384]{2,1,0:T(8,128)}) %reduce-scatter.3.cloned.1.call-update) | async-done | bytes 1179664 | tf_op jit(solution)/shard_map/reduce_scatter | solution.py:266
  3100.0 8.8 copy.1519
  (3648 shorter events, 1544.5 us)
Async XLA Ops:
  7.2 992.9 %all-gather.15.cloned.1.call-start = ((), (), s32[]{:S(2)}) async-start(), calls=%async_computation.11 | async-start | bytes 3244032 | tf_op jit(solution)/shard_map/all_gather | solution.py:40
  16.8 9.4 collective-permute-start
  113.8 107.9 %copy-start.104 = (f32[4,32,16]{2,1,0:T(8,128)S(1)}, f32[4,32,16]{2,1,0:T(8,128)}, u32[]{:S(2)}) copy-start(f32[4,32,16]{2,1,0:T(8,128)} %copy-done.103) | copy-start | bytes 24580 | tf_op jit(solution)/shard_map/jvp()/while
  113.8 107.9 %copy-start.194 = (f32[4,1,16]{2,1,0:T(1,128)S(1)}, f32[4,1,16]{2,1,0:T(1,128)}, u32[]{:S(2)}) copy-start(f32[4,1,16]{2,1,0:T(1,128)} %copy-done.193) | copy-start | bytes 772 | tf_op jit(solution)/shard_map/jvp()/while
  117.4 104.2 %copy-start.216 = (f32[4]{0:T(128)}, f32[4]{0:T(128)S(1)}, u32[]{:S(2)}) copy-start(f32[4]{0:T(128)S(1)} %get-tuple-element.21621) | copy-start | bytes 52 | tf_op jit(solution)/shard_map/jvp()/while
  117.4 104.2 %copy-start.223 = (f32[4]{0:T(128)}, f32[4]{0:T(128)S(1)}, u32[]{:S(2)}) copy-start(f32[4]{0:T(128)S(1)} %get-tuple-element.21632) | copy-start | bytes 52 | tf_op jit(solution)/shard_map/jvp()/while
  117.5 104.1 %copy-start.227 = (f32[4]{0:T(128)}, f32[4]{0:T(128)S(1)}, u32[]{:S(2)}) copy-start(f32[4]{0:T(128)S(1)} %get-tuple-element.21642) | copy-start | bytes 52 | tf_op jit(solution)/shard_map/jvp()/while
  117.5 104.1 %copy-start.229 = (f32[4]{0:T(128)}, f32[4]{0:T(128)S(1)}, u32[]{:S(2)}) copy-start(f32[4]{0:T(128)S(1)} %get-tuple-element.21652) | copy-start | bytes 52 | tf_op jit(solution)/shard_map/jvp()/while
  298.9 107.9 %copy-start.104 = (f32[4,32,16]{2,1,0:T(8,128)S(1)}, f32[4,32,16]{2,1,0:T(8,128)}, u32[]{:S(2)}) copy-start(f32[4,32,16]{2,1,0:T(8,128)} %copy-done.103) | copy-start | bytes 24580 | tf_op jit(solution)/shard_map/jvp()/while
  298.9 107.9 %copy-start.194 = (f32[4,1,16]{2,1,0:T(1,128)S(1)}, f32[4,1,16]{2,1,0:T(1,128)}, u32[]{:S(2)}) copy-start(f32[4,1,16]{2,1,0:T(1,128)} %copy-done.193) | copy-start | bytes 772 | tf_op jit(solution)/shard_map/jvp()/while
  302.5 104.1 %copy-start.216 = (f32[4]{0:T(128)}, f32[4]{0:T(128)S(1)}, u32[]{:S(2)}) copy-start(f32[4]{0:T(128)S(1)} %get-tuple-element.21621) | copy-start | bytes 52 | tf_op jit(solution)/shard_map/jvp()/while
  302.6 104.1 %copy-start.223 = (f32[4]{0:T(128)}, f32[4]{0:T(128)S(1)}, u32[]{:S(2)}) copy-start(f32[4]{0:T(128)S(1)} %get-tuple-element.21632) | copy-start | bytes 52 | tf_op jit(solution)/shard_map/jvp()/while
  302.6 104.0 %copy-start.227 = (f32[4]{0:T(128)}, f32[4]{0:T(128)S(1)}, u32[]{:S(2)}) copy-start(f32[4]{0:T(128)S(1)} %get-tuple-element.21642) | copy-start | bytes 52 | tf_op jit(solution)/shard_map/jvp()/while
  483.9 108.0 %copy-start.104 = (f32[4,32,16]{2,1,0:T(8,128)S(1)}, f32[4,32,16]{2,1,0:T(8,128)}, u32[]{:S(2)}) copy-start(f32[4,32,16]{2,1,0:T(8,128)} %copy-done.103) | copy-start | bytes 24580 | tf_op jit(solution)/shard_map/jvp()/while
  483.9 108.0 %copy-start.194 = (f32[4,1,16]{2,1,0:T(1,128)S(1)}, f32[4,1,16]{2,1,0:T(1,128)}, u32[]{:S(2)}) copy-start(f32[4,1,16]{2,1,0:T(1,128)} %copy-done.193) | copy-start | bytes 772 | tf_op jit(solution)/shard_map/jvp()/while
  487.5 104.2 %copy-start.216 = (f32[4]{0:T(128)}, f32[4]{0:T(128)S(1)}, u32[]{:S(2)}) copy-start(f32[4]{0:T(128)S(1)} %get-tuple-element.21621) | copy-start | bytes 52 | tf_op jit(solution)/shard_map/jvp()/while
  487.5 104.2 %copy-start.223 = (f32[4]{0:T(128)}, f32[4]{0:T(128)S(1)}, u32[]{:S(2)}) copy-start(f32[4]{0:T(128)S(1)} %get-tuple-element.21632) | copy-start | bytes 52 | tf_op jit(solution)/shard_map/jvp()/while
  487.6 104.1 %copy-start.227 = (f32[4]{0:T(128)}, f32[4]{0:T(128)S(1)}, u32[]{:S(2)}) copy-start(f32[4]{0:T(128)S(1)} %get-tuple-element.21642) | copy-start | bytes 52 | tf_op jit(solution)/shard_map/jvp()/while
  487.6 104.1 %copy-start.229 = (f32[4]{0:T(128)}, f32[4]{0:T(128)S(1)}, u32[]{:S(2)}) copy-start(f32[4]{0:T(128)S(1)} %get-tuple-element.21652) | copy-start | bytes 52 | tf_op jit(solution)/shard_map/jvp()/while
  668.9 108.0 %copy-start.104 = (f32[4,32,16]{2,1,0:T(8,128)S(1)}, f32[4,32,16]{2,1,0:T(8,128)}, u32[]{:S(2)}) copy-start(f32[4,32,16]{2,1,0:T(8,128)} %copy-done.103) | copy-start | bytes 24580 | tf_op jit(solution)/shard_map/jvp()/while
  668.9 108.0 %copy-start.194 = (f32[4,1,16]{2,1,0:T(1,128)S(1)}, f32[4,1,16]{2,1,0:T(1,128)}, u32[]{:S(2)}) copy-start(f32[4,1,16]{2,1,0:T(1,128)} %copy-done.193) | copy-start | bytes 772 | tf_op jit(solution)/shard_map/jvp()/while
  672.6 104.2 %copy-start.216 = (f32[4]{0:T(128)}, f32[4]{0:T(128)S(1)}, u32[]{:S(2)}) copy-start(f32[4]{0:T(128)S(1)} %get-tuple-element.21621) | copy-start | bytes 52 | tf_op jit(solution)/shard_map/jvp()/while
  672.6 104.2 %copy-start.223 = (f32[4]{0:T(128)}, f32[4]{0:T(128)S(1)}, u32[]{:S(2)}) copy-start(f32[4]{0:T(128)S(1)} %get-tuple-element.21632) | copy-start | bytes 52 | tf_op jit(solution)/shard_map/jvp()/while
  672.7 104.1 %copy-start.227 = (f32[4]{0:T(128)}, f32[4]{0:T(128)S(1)}, u32[]{:S(2)}) copy-start(f32[4]{0:T(128)S(1)} %get-tuple-element.21642) | copy-start | bytes 52 | tf_op jit(solution)/shard_map/jvp()/while
  672.7 104.1 %copy-start.229 = (f32[4]{0:T(128)}, f32[4]{0:T(128)S(1)}, u32[]{:S(2)}) copy-start(f32[4]{0:T(128)S(1)} %get-tuple-element.21652) | copy-start | bytes 52 | tf_op jit(solution)/shard_map/jvp()/while
  778.0 227.5 %all-gather.13.cloned.1.call-start = ((), (), s32[]{:S(2)}) async-start(), calls=%async_computation.10 | async-start | bytes 3244032 | tf_op jit(solution)/shard_map/all_gather | solution.py:40
  778.7 353.1 %all-gather.9.cloned.1.call-start = ((), (), s32[]{:S(2)}) async-start(), calls=%async_computation.6 | async-start | bytes 10616832 | tf_op jit(solution)/shard_map/all_gather | solution.py:220
  779.5 485.7 %all-gather.11.cloned.1.call-start = ((), (), s32[]{:S(2)}) async-start(), calls=%async_computation.7 | async-start | bytes 10616832 | tf_op jit(solution)/shard_map/all_gather | solution.py:248
  779.5 33.8 %collective-permute-start.1 = (f32[1,384,768]{2,1,0:T(8,128)}, f32[1,384,768]{2,1,0:T(8,128)S(1)}, u32[]{:S(2)}, u32[]{:S(2)}) collective-permute-start(f32[1,384,768]{2,1,0:T(8,128)} %param.47), channel_id=1, source_target_pairs={{0,4},{4,8},{8,12},{12,16},{16,20},{20,24},{24,28},{28,0},{1,5},{5... | collective-permute-start | bytes 3538952 | tf_op jit(solution)/shard_map/ppermute | solution.py:23
  814.3 60.0 %collective-permute-start.2 = (f32[1,384,768]{2,1,0:T(8,128)S(1)}, f32[1,384,768]{2,1,0:T(8,128)S(1)}, u32[]{:S(2)}, u32[]{:S(2)}) collective-permute-start(f32[1,384,768]{2,1,0:T(8,128)S(1)} %collective-permute-done.1), channel_id=1, source_target_pairs={{0,4},{4,8},{8,12},{12,16},{16,20},{20,24},{24,28},{28,0},{1,5},{5... | collective-permute-start | bytes 3538952 | tf_op jit(solution)/shard_map/ppermute | solution.py:23
  814.4 63.8 %collective-permute-start.5 = (f32[1,384,768]{2,1,0:T(8,128)}, f32[1,384,768]{2,1,0:T(8,128)}, u32[]{:S(2)}, u32[]{:S(2)}) collective-permute-start(f32[1,384,768]{2,1,0:T(8,128)} %param.47), channel_id=1, source_target_pairs={{4,0},{8,4},{12,8},{16,12},{20,16},{24,20},{28,24},{0,28},{5,1},{9... | collective-permute-start | bytes 3538952 | tf_op jit(solution)/shard_map/ppermute | solution.py:25
  874.4 56.8 %collective-permute-start.3 = (f32[1,384,768]{2,1,0:T(8,128)S(1)}, f32[1,384,768]{2,1,0:T(8,128)}, u32[]{:S(2)}, u32[]{:S(2)}) collective-permute-start(f32[1,384,768]{2,1,0:T(8,128)S(1)} %collective-permute-done.2), channel_id=1, source_target_pairs={{0,4},{4,8},{8,12},{12,16},{16,20},{20,24},{24,28},{28,0},{1,5},{5... | collective-permute-start | bytes 3538952 | tf_op jit(solution)/shard_map/ppermute | solution.py:23
  878.2 65.1 %collective-permute-start.6 = (f32[1,384,768]{2,1,0:T(8,128)}, f32[1,384,768]{2,1,0:T(8,128)}, u32[]{:S(2)}, u32[]{:S(2)}) collective-permute-start(f32[1,384,768]{2,1,0:T(8,128)} %collective-permute-done.5), channel_id=1, source_target_pairs={{4,0},{8,4},{12,8},{16,12},{20,16},{24,20},{28,24},{0,28},{5,1},{9... | collective-permute-start | bytes 3538952 | tf_op jit(solution)/shard_map/ppermute | solution.py:25
  931.1 58.5 %collective-permute-start.4 = (f32[1,384,768]{2,1,0:T(8,128)}, f32[1,384,768]{2,1,0:T(8,128)}, u32[]{:S(2)}, u32[]{:S(2)}) collective-permute-start(f32[1,384,768]{2,1,0:T(8,128)} %collective-permute-done.3), channel_id=1, source_target_pairs={{0,4},{4,8},{8,12},{12,16},{16,20},{20,24},{24,28},{28,0},{1,5},{5... | collective-permute-start | bytes 3538952 | tf_op jit(solution)/shard_map/ppermute | solution.py:23
  943.3 176.8 %collective-permute-start.7 = (f32[1,384,768]{2,1,0:T(8,128)}, f32[1,384,768]{2,1,0:T(8,128)}, u32[]{:S(2)}, u32[]{:S(2)}) collective-permute-start(f32[1,384,768]{2,1,0:T(8,128)} %collective-permute-done.6), channel_id=1, source_target_pairs={{4,0},{8,4},{12,8},{16,12},{20,16},{24,20},{28,24},{0,28},{5,1},{9... | collective-permute-start | bytes 3538952 | tf_op jit(solution)/shard_map/ppermute | solution.py:25
  1111.9 194.0 %copy-start.154 = (f32[128]{0:T(128)}, f32[128]{0:T(128)S(1)}, u32[]{:S(2)}) copy-start(f32[128]{0:T(128)S(1)} %fusion.683) | copy-start | bytes 1540
  1114.0 17.0 all-to-all-start
  1140.5 124.6 %copy-start.3 = (f32[4,1,40,3072]{3,2,0,1:T(8,128)}, f32[4,1,40,3072]{3,2,0,1:T(8,128)S(1)}, u32[]{:S(2)}) copy-start(f32[4,1,40,3072]{3,2,0,1:T(8,128)S(1)} %fusion.584) | copy-start | bytes 5898244
  1148.1 12.9 all-to-all-start.1
  1154.0 142.7 %copy-start.134 = (f32[128,4]{0,1:T(4,128)}, f32[128,4]{0,1:T(4,128)S(1)}, u32[]{:S(2)}) copy-start(f32[128,4]{0,1:T(4,128)S(1)} %get-tuple-element.14993) | copy-start | bytes 6148
  1154.0 142.7 %copy-start.156 = (f32[128]{0:T(128)}, f32[128]{0:T(128)S(1)}, u32[]{:S(2)}) copy-start(f32[128]{0:T(128)S(1)} %get-tuple-element.14992) | copy-start | bytes 1540
  1168.4 96.8 %all-to-all-start.2 = ((f32[4,40,768]{2,1,0:T(8,128)}), f32[4,40,768]{2,1,0:T(8,128)}, u32[]{:S(2)}, u32[]{:S(2)}) async-start(f32[4,40,768]{2,1,0:T(8,128)} %bitcast.2493), calls=%async_computation.2 | async-start | bytes 983040 | tf_op jit(solution)/shard_map/all_to_all | solution.py:245
  1292.6 12.1 all-to-all-start.3
  1296.2 103.6 %all-gather.17.cloned.1.call-start = ((), (), s32[]{:S(2)}) async-start(), calls=%async_computation.12 | async-start | bytes 3244032 | tf_op jit(solution)/shard_map/all_gather | solution.py:40
  1343.3 1419.3 %all-reduce.178.cloned.1.call-start = ((), (), s32[]{:S(2)}) async-start(), calls=%async_computation.13 | async-start | bytes 30081024 | tf_op jit(solution)/shard_map/psum | solution.py:308
  2204.5 3.1 collective-permute-start.8
  2217.8 715.6 %reduce-scatter.5.cloned.1.call-start = ((), (), s32[]{:S(2)}) async-start(), calls=%async_computation.9 | async-start | bytes 10616832 | tf_op jit(solution)/shard_map/reduce_scatter | solution.py:267
  2230.8 869.2 %reduce-scatter.3.cloned.1.call-start = ((), (), s32[]{:S(2)}) async-start(), calls=%async_computation.8 | async-start | bytes 10616832 | tf_op jit(solution)/shard_map/reduce_scatter | solution.py:266
  (590 other events, 16849.1 us)
Sparse Core Ops, SparseCore 0:
  778.1 105.7 all-gather.14
  887.4 91.5 all-gather.12
  981.1 145.8 all-gather.8
  1129.0 136.1 all-gather.10
  1343.4 56.3 all-gather.16
  2218.0 544.5 all-reduce.177
  2768.6 164.7 reduce-scatter.4
  2937.6 162.3 reduce-scatter.2
